TPU v7x, 128 devices: a whole 4x4x4 slice. The times are simulated.
128 devices in a mesh: group: 4 (over z_lo, core), dp: 2 (over z_hi), tensor: 16 (over x, y).
Axes of the slice: x: 4, y: 4, z: 4 (z_hi: 2, z_lo: 2; z = z_hi * 2 + z_lo), core: 2. Of those that a mesh axis runs over, the one named last changes fastest.
Arguments:
- tokens: bfloat16 [2048, 8, 2048], P('tensor', ('group', 'dp')), may hold values from -6 to 6
- cotangent: bfloat16 [2048, 8, 2048], P('tensor', ('group', 'dp')), may hold values from -6 to 6
- lengths: int32 [8], replicated, may hold values from 1 to 2048, 9830 in all
- ln1_gain: float32 [2048], replicated, may hold values from 0.25 to 1.75
- ln1_bias: float32 [2048], replicated, may hold values from -1.75 to 1.75
- w_qkv: bfloat16 [2048, 3, 16, 128], P(None, None, 'tensor'), may hold values from -0.125 to 0.125
- b_qv: float32 [2, 2048], P(None, 'tensor'), may hold values from -1.75 to 1.75
- w_o: bfloat16 [16, 128, 2048], P('tensor'), may hold values from -0.75 to 0.75
- b_o: float32 [2048], replicated, may hold values from -1.75 to 1.75
- ln2_gain: float32 [2048], replicated, may hold values from 0.25 to 1.75
- ln2_bias: float32 [2048], replicated, may hold values from -1.75 to 1.75
- w_in: bfloat16 [2048, 8192], P(None, 'tensor'), may hold values from -0.125 to 0.125
- b_in: float32 [8192], P('tensor'), may hold values from -1.75 to 1.75
- w_out: bfloat16 [8192, 2048], P('tensor'), may hold values from -0.0625 to 0.0625
- b_out: float32 [2048], replicated, may hold values from -1.75 to 1.75
Outputs:
- output: bfloat16 [2048, 8, 2048], P('tensor', ('group', 'dp'))
- input_grad: bfloat16 [2048, 8, 2048], P('tensor', ('group', 'dp'))
- d_ln1_gain: float32 [2048], P(('group', 'dp', 'tensor'))
- d_ln1_bias: float32 [2048], P(('group', 'dp', 'tensor'))
- d_w_qkv: float32 [2048, 3, 16, 128], P(('group', 'dp'), None, 'tensor')
- d_b_qv: float32 [2, 2048], P(None, ('group', 'dp', 'tensor'))
- d_w_o: float32 [16, 128, 2048], P('tensor', None, ('group', 'dp'))
- d_b_o: float32 [2048], P(('group', 'dp', 'tensor'))
- d_ln2_gain: float32 [2048], P(('group', 'dp', 'tensor'))
- d_ln2_bias: float32 [2048], P(('group', 'dp', 'tensor'))
- d_w_in: float32 [2048, 8192], P(('group', 'dp'), 'tensor')
- d_b_in: float32 [8192], P(('group', 'dp', 'tensor'))
- d_w_out: float32 [8192, 2048], P('tensor', ('group', 'dp'))
- d_b_out: float32 [2048], P(('group', 'dp', 'tensor'))
Inputs may be any that keep to these rules, and one draw needn't show every extreme that they name: The true lengths of the 8 sequences sum to 9830.
All inputs are finite; a program needn't handle non-finite values.
Results may differ from a plain program's by a relative error of at most 0.02.
Values may be sent and summed in bfloat16 or wider, within the bound.
No kernel may reach another device: no remote copies, remote signals or barrier semaphores. Data moves between devices by JAX's collectives and lax.ppermute only.
A program may use at most 192 MiB of HBM per device.

v0:
```python
from functools import partial
import math
import jax
import jax.numpy as jnp
from jax import lax
from jax.sharding import PartitionSpec as P

EPS = 1e-05
NEGATIVE = -1e30


def layer_norm(value, gain, shift):
    mean = jnp.mean(value, axis=-1, keepdims=True)
    centred = value - mean
    spread = jnp.mean(centred * centred, axis=-1, keepdims=True)
    return centred * lax.rsqrt(spread + EPS) * gain + shift


def gelu_tanh(value):
    return jax.nn.gelu(value, approximate=True)


def block_scores(rows_query, key_rows, first, length, score_scale):
    count = rows_query.shape[0]
    key_pos = jnp.arange(key_rows.shape[0], dtype=jnp.int32)
    query_pos = first + jnp.arange(count, dtype=jnp.int32)
    valid = (key_pos[None, :] <= query_pos[:, None]) & (key_pos[None, :] < length)
    scores = (
        lax.dot_general(
            rows_query, key_rows, (((1,), (1,)), ((), ())), preferred_element_type=jnp.float32
        )
        * score_scale
    )
    return (jnp.where(valid, scores, NEGATIVE), valid)


def attend_forward(item, block_rows, score_scale):
    query, key_rows, value_rows, length = item
    outputs = []
    log_parts = []
    for first in range(0, query.shape[0], block_rows):
        rows_query = query[first : first + block_rows]
        scores, valid = block_scores(rows_query, key_rows, first, length, score_scale)
        peak = jnp.max(scores, axis=-1, keepdims=True)
        expo = jnp.exp(scores - peak)
        weight_sum = jnp.sum(expo, axis=-1, keepdims=True)
        probs = (expo / weight_sum).astype(jnp.bfloat16)
        outputs.append(
            jnp.dot(probs, value_rows, preferred_element_type=jnp.float32).astype(jnp.bfloat16)
        )
        log_parts.append((peak + jnp.log(weight_sum))[:, 0])
    return (jnp.concatenate(outputs, 0), jnp.concatenate(log_parts, 0))


def attend_backward(item, block_rows, score_scale):
    query, key_rows, value_rows, length, grad_out, log_sums = item
    key_grad = jnp.zeros(key_rows.shape, jnp.float32)
    value_grad = jnp.zeros(value_rows.shape, jnp.float32)
    query_parts = []
    for first in range(0, query.shape[0], block_rows):
        rows_query = query[first : first + block_rows]
        scores, valid = block_scores(rows_query, key_rows, first, length, score_scale)
        probs = jnp.where(valid, jnp.exp(scores - log_sums[first : first + block_rows, None]), 0.0)
        grad_rows = grad_out[first : first + block_rows]
        probs_grad = lax.dot_general(
            grad_rows, value_rows, (((1,), (1,)), ((), ())), preferred_element_type=jnp.float32
        )
        inner = jnp.sum(probs * probs_grad, axis=-1, keepdims=True)
        score_grad = (probs * (probs_grad - inner)).astype(jnp.bfloat16)
        query_parts.append(
            jnp.dot(score_grad, key_rows, preferred_element_type=jnp.float32) * score_scale
        )
        key_grad = (
            key_grad
            + lax.dot_general(
                score_grad, rows_query, (((0,), (0,)), ((), ())), preferred_element_type=jnp.float32
            )
            * score_scale
        )
        value_grad = value_grad + lax.dot_general(
            probs.astype(jnp.bfloat16),
            grad_rows,
            (((0,), (0,)), ((), ())),
            preferred_element_type=jnp.float32,
        )
    return (
        jnp.concatenate(query_parts, 0).astype(jnp.bfloat16),
        key_grad.astype(jnp.bfloat16),
        value_grad.astype(jnp.bfloat16),
    )


def shards(
    tokens,
    cotangent,
    lengths,
    ln1_gain,
    ln1_bias,
    w_qkv,
    b_qv,
    w_o,
    b_o,
    ln2_gain,
    ln2_bias,
    w_in,
    b_in,
    w_out,
    b_out,
):
    row_count, seq_count, model_width = tokens.shape
    tensor_count = lax.axis_size("tensor")
    tensor_rank = lax.axis_index("tensor")
    seq_total = row_count * tensor_count
    local_heads = w_qkv.shape[2]
    head_size = w_qkv.shape[3]
    local_width = local_heads * head_size
    hidden = w_in.shape[1]
    block_rows = min(512, seq_total)
    score_scale = 1.0 / math.sqrt(head_size)
    group_count = lax.axis_size("group")
    group_rank = lax.axis_index("group")
    member = group_rank * lax.axis_size("dp") + lax.axis_index("dp")
    seq_lengths = lax.dynamic_slice_in_dim(lengths, member * seq_count, seq_count, 0)
    group_totals = jnp.sum(lengths.reshape(group_count, -1), axis=1).astype(jnp.float32)
    factor = (
        group_count
        * lax.dynamic_index_in_dim(group_totals, group_rank, 0, keepdims=False)
        / jnp.sum(group_totals)
    )
    inputs = tokens.astype(jnp.float32)
    normed_low = layer_norm(inputs, ln1_gain, ln1_bias).astype(jnp.bfloat16)
    normed_full = lax.all_gather(normed_low, "tensor", axis=0, tiled=True)
    joint_weight = w_qkv.reshape(model_width, 3 * local_width)
    projected = jnp.dot(
        normed_full.reshape(seq_total * seq_count, model_width),
        joint_weight,
        preferred_element_type=jnp.float32,
    )
    projected = projected.reshape(seq_total, seq_count, 3, local_width)
    query = (projected[:, :, 0] + b_qv[0]).astype(jnp.bfloat16)
    keys = projected[:, :, 1].astype(jnp.bfloat16)
    values = (projected[:, :, 2] + b_qv[1]).astype(jnp.bfloat16)

    def per_item(array):
        shaped = array.reshape(seq_total, seq_count, local_heads, head_size)
        return jnp.transpose(shaped, (1, 2, 0, 3)).reshape(
            seq_count * local_heads, seq_total, head_size
        )

    def per_row(array):
        shaped = array.reshape(seq_count, local_heads, seq_total, head_size)
        return jnp.transpose(shaped, (2, 0, 1, 3)).reshape(seq_total, seq_count, local_width)

    query_items = per_item(query)
    key_items = per_item(keys)
    value_items = per_item(values)
    item_lengths = jnp.repeat(seq_lengths, local_heads)
    heads_out, log_sums = lax.map(
        partial(attend_forward, block_rows=block_rows, score_scale=score_scale),
        (query_items, key_items, value_items, item_lengths),
    )
    attended = per_row(heads_out)
    out_weight = w_o.reshape(local_width, model_width)
    positions = tensor_rank * row_count + jnp.arange(row_count, dtype=jnp.int32)
    live = positions[:, None] < seq_lengths[None, :]
    upstream = jnp.where(live[:, :, None], cotangent, jnp.zeros_like(cotangent))
    upstream_full = lax.all_gather(upstream, "tensor", axis=0, tiled=True)
    attention_part = jnp.einsum(
        "rse,ed->rsd", attended, out_weight, preferred_element_type=jnp.float32
    ).astype(jnp.bfloat16)
    attention_part, upstream_full = lax.optimization_barrier((attention_part, upstream_full))
    attention = (
        lax.psum_scatter(attention_part, "tensor", scatter_dimension=0, tiled=True).astype(
            jnp.float32
        )
        + b_o
    )
    middle = inputs + attention
    second_low = layer_norm(middle, ln2_gain, ln2_bias).astype(jnp.bfloat16)
    second_full = lax.all_gather(second_low, "tensor", axis=0, tiled=True)
    pre_act = (
        jnp.dot(
            second_full.reshape(seq_total * seq_count, model_width),
            w_in,
            preferred_element_type=jnp.float32,
        )
        + b_in
    )
    activated = gelu_tanh(pre_act).astype(jnp.bfloat16).reshape(seq_total, seq_count, hidden)
    feed_part = jnp.einsum(
        "rsf,fd->rsd", activated, w_out, preferred_element_type=jnp.float32
    ).astype(jnp.bfloat16)
    piece = upstream_full
    weight_grad = jnp.einsum("rsf,rsd->fd", activated, piece, preferred_element_type=jnp.float32)
    part = jnp.einsum("rsd,fd->rsf", piece, w_out, preferred_element_type=jnp.float32)
    act_grad = part
    grad_w_out = weight_grad
    gelu_back = jax.vjp(gelu_tanh, pre_act)[1]
    pre_low = gelu_back(act_grad.reshape(seq_total * seq_count, hidden))[0].astype(jnp.bfloat16)
    grad_b_in = jnp.sum(pre_low, axis=0, dtype=jnp.float32)
    grad_w_in = jnp.einsum(
        "rd,rf->df",
        second_full.reshape(seq_total * seq_count, model_width),
        pre_low,
        preferred_element_type=jnp.float32,
    )
    pre_rows = pre_low.reshape(seq_total, seq_count, hidden)
    piece = pre_rows
    second_grad = lax.psum_scatter(
        jnp.einsum("rsf,df->rsd", piece, w_in, preferred_element_type=jnp.float32).astype(
            jnp.bfloat16
        ),
        "tensor",
        scatter_dimension=0,
        tiled=True,
    ).astype(jnp.float32)
    norm_two_back = jax.vjp(layer_norm, middle, ln2_gain, ln2_bias)[1]
    middle_part, grad_ln2_gain, grad_ln2_bias = norm_two_back(second_grad)
    middle_grad = upstream.astype(jnp.float32) + middle_part
    branch_low = middle_grad.astype(jnp.bfloat16)
    grad_b_o = jnp.sum(branch_low, axis=(0, 1), dtype=jnp.float32)
    grad_b_out = jnp.sum(upstream, axis=(0, 1), dtype=jnp.float32)
    piece = lax.all_gather(branch_low, "tensor", axis=0, tiled=True)
    feed_part, piece = lax.optimization_barrier((feed_part, piece))
    feed = (
        lax.psum_scatter(feed_part, "tensor", scatter_dimension=0, tiled=True).astype(jnp.float32)
        + b_out
    )
    output = (middle + feed).astype(jnp.bfloat16)
    weight_grad = jnp.einsum("rse,rsd->ed", attended, piece, preferred_element_type=jnp.float32)
    part = jnp.einsum("rsd,ed->rse", piece, out_weight, preferred_element_type=jnp.float32)
    head_items = per_item(part.astype(jnp.bfloat16))
    grads_query, grads_keys, grads_values = lax.map(
        partial(attend_backward, block_rows=block_rows, score_scale=score_scale),
        (query_items, key_items, value_items, item_lengths, head_items, log_sums),
    )
    joint_grad = jnp.stack(
        (per_row(grads_query), per_row(grads_keys), per_row(grads_values)), axis=2
    )
    grad_b_qv = jnp.sum(joint_grad[:, :, 0::2], axis=(0, 1), dtype=jnp.float32)
    joint_rows = joint_grad.reshape(seq_total, seq_count, 3 * local_width)
    grad_w_qkv = jnp.einsum(
        "rd,rc->dc",
        normed_full.reshape(seq_total * seq_count, model_width),
        joint_rows.reshape(seq_total * seq_count, 3 * local_width),
        preferred_element_type=jnp.float32,
    )
    piece = joint_rows
    normed_grad = lax.psum_scatter(
        jnp.einsum("rsc,dc->rsd", piece, joint_weight, preferred_element_type=jnp.float32).astype(
            jnp.bfloat16
        ),
        "tensor",
        scatter_dimension=0,
        tiled=True,
    ).astype(jnp.float32)
    norm_one_back = jax.vjp(layer_norm, inputs, ln1_gain, ln1_bias)[1]
    input_part, grad_ln1_gain, grad_ln1_bias = norm_one_back(normed_grad)
    input_grad = (middle_grad + input_part).astype(jnp.bfloat16)
    summed = (
        halving_sum(grad_w_qkv.reshape(model_width, 3, local_heads, head_size) * factor, 0),
        halving_sum(weight_grad.reshape(local_heads, head_size, model_width) * factor, 2),
        halving_sum(grad_w_in * factor, 0),
        halving_sum(grad_w_out * factor, 1),
    )
    in_full = lax.dynamic_update_slice_in_dim(
        jnp.zeros((hidden * tensor_count,), jnp.float32), grad_b_in, tensor_rank * hidden, 0
    )
    joint_full = lax.dynamic_update_slice_in_dim(
        jnp.zeros((2, local_width * tensor_count), jnp.float32),
        grad_b_qv,
        tensor_rank * local_width,
        1,
    )
    shard_count = group_count * lax.axis_size("dp")
    vectors = (
        grad_ln1_gain,
        grad_ln1_bias,
        grad_b_o,
        grad_ln2_gain,
        grad_ln2_bias,
        grad_b_out,
        joint_full[0],
        joint_full[1],
        in_full,
    )
    pieces = [
        jnp.transpose((item * factor).reshape(shard_count, tensor_count, -1), (1, 0, 2))
        for item in vectors
    ]
    widths = [piece.shape[2] for piece in pieces]
    packed = jnp.concatenate(pieces, 2)
    packed = halving_steps(
        packed,
        0,
        [
            ("tensor", tensor_count, 8),
            ("tensor", tensor_count, 4),
            ("tensor", tensor_count, 2),
            ("tensor", tensor_count, 1),
        ],
    )
    packed = halving_steps(
        packed,
        1,
        [("group", group_count, 2), ("group", group_count, 1), ("dp", lax.axis_size("dp"), 1)],
    )
    flat = packed.reshape(-1)
    parts = []
    offset = 0
    for width in widths:
        parts.append(flat[offset : offset + width])
        offset += width
    return (
        output,
        input_grad,
        parts[0],
        parts[1],
        summed[0],
        jnp.stack((parts[6], parts[7])),
        summed[1],
        parts[2],
        parts[3],
        parts[4],
        summed[2],
        parts[8],
        summed[3],
        parts[5],
    )


def halving_steps(value, dim, steps, send_type=None):
    for axis, size, bit in steps:
        half = value.shape[dim] // 2
        low_half = lax.slice_in_dim(value, 0, half, axis=dim)
        high_half = lax.slice_in_dim(value, half, 2 * half, axis=dim)
        upper = lax.axis_index(axis) // bit % 2 == 1
        keep = jnp.where(upper, high_half, low_half)
        send = jnp.where(upper, low_half, high_half)
        if send_type is not None:
            send = send.astype(send_type)
        got = lax.ppermute(send, axis, [(i, i ^ bit) for i in range(size)])
        value = keep + got.astype(keep.dtype)
    return value


def halving_sum(value, dim):
    shape = value.shape
    groups = lax.axis_size("group")
    dps = lax.axis_size("dp")
    split = shape[:dim] + (groups * dps, shape[dim] // (groups * dps)) + shape[dim + 1 :]
    value = value.reshape(split)
    value = halving_steps(
        value, dim, [("group", groups, 2), ("group", groups, 1), ("dp", dps, 1)], jnp.bfloat16
    )
    return value.reshape(shape[:dim] + (shape[dim] // (groups * dps),) + shape[dim + 1 :])


def solution(mesh):
    in_specs = (
        P("tensor", ("group", "dp"), None),
        P("tensor", ("group", "dp"), None),
        P(),
        P(),
        P(),
        P(None, None, "tensor", None),
        P(None, "tensor"),
        P("tensor", None, None),
        P(),
        P(),
        P(),
        P(None, "tensor"),
        P("tensor"),
        P("tensor", None),
        P(),
    )
    out_specs = (
        P("tensor", ("group", "dp"), None),
        P("tensor", ("group", "dp"), None),
        P(("group", "dp", "tensor")),
        P(("group", "dp", "tensor")),
        P(("group", "dp"), None, "tensor", None),
        P(None, ("group", "dp", "tensor")),
        P("tensor", None, ("group", "dp")),
        P(("group", "dp", "tensor")),
        P(("group", "dp", "tensor")),
        P(("group", "dp", "tensor")),
        P(("group", "dp"), "tensor"),
        P(("group", "dp", "tensor")),
        P("tensor", ("group", "dp")),
        P(("group", "dp", "tensor")),
    )
    return jax.shard_map(shards, mesh=mesh, in_specs=in_specs, out_specs=out_specs, check_vma=False)
```

profile of v0, /device:TPU:0, one launch (start us, length us, event | category | flops | bytes accessed | tf_op | source)
XLA Modules:
  0.0 779.4 jit_solution(8731599573753859071)
XLA Ops:
  20.3 65.2 %all-gather.5.cloned.1.call-done = bf16[2048,1,2048]{2,0,1:T(8,128)(2,1)} async-done(((bf16[128,1,2048]{2,0,1:T(8,128)(2,1)}), bf16[2048,1,2048]{2,0,1:T(8,128)(2,1)}) %all-gather.5.cloned.1.call-update) | async-done | bytes 8388624 | tf_op jit(solution)/shard_map/all_gather | solution.py:132
  85.5 7.4 fusion.33
  98.0 4.2 online-softmax.3
  103.2 5.2 fusion.126
  113.4 5.2 fusion.125
  123.6 4.8 fusion.124
  128.4 4.4 online-softmax
  133.8 5.6 convert_bitcast_fusion.3
  139.4 19.1 %all-gather.7.cloned.1.call-done = bf16[2048,1,2048]{2,0,1:T(8,128)(2,1)} async-done(((bf16[128,1,2048]{2,0,1:T(8,128)(2,1)}), bf16[2048,1,2048]{2,0,1:T(8,128)(2,1)}) %all-gather.7.cloned.1.call-update) | async-done | bytes 8388624 | tf_op jit(solution)/shard_map/all_gather | solution.py:167
  158.6 88.1 %reduce-scatter.5.cloned.1.call-done = bf16[128,1,2048]{2,0,1:T(8,128)(2,1)} async-done(((bf16[2048,1,2048]{2,0,1:T(8,128)(2,1)}), bf16[128,1,2048]{2,0,1:T(8,128)(2,1)}) %reduce-scatter.5.cloned.1.call-update) | async-done | bytes 524304 | tf_op jit(solution)/shard_map/reduce_scatter | solution.py:173
  251.7 70.2 %all-gather.9.cloned.1.call-done = bf16[2048,1,2048]{2,0,1:T(8,128)(2,1)} async-done(((bf16[128,1,2048]{2,0,1:T(8,128)(2,1)}), bf16[2048,1,2048]{2,0,1:T(8,128)(2,1)}) %all-gather.9.cloned.1.call-update) | async-done | bytes 8388624 | tf_op jit(solution)/shard_map/all_gather | solution.py:180
  321.9 7.5 fusion.10
  329.4 13.1 %convert_reduce_fusion = (f32[512]{0:T(512)}, bf16[2048,512]{1,0:T(8,128)(2,1)S(1)}) fusion(f32[2048,512]{1,0:T(8,128)S(1)} %fusion.10, f32[512]{0:T(512)S(1)} %copy-done.85, bf16[512,2048]{1,0:T(8,128)(2,1)S(1)} %copy-done, bf16[2048,1,2048]{2,0,1:T(8,128)(2,1)} %all-gather.7.cloned.1.call-done), kind=kOutput, calls=%fused_computation.29 | convolution fusion | flops 4319084032 | bytes 16781312 | tf_op jit(solution)/shard_map/rsd,fd->rsf/dot_general | solution.py:195
  343.9 6.9 convert_bitcast_fusion.1
  350.9 84.8 %reduce-scatter.7.cloned.1.call-done = bf16[128,1,2048]{2,0,1:T(8,128)(2,1)} async-done(((bf16[2048,1,2048]{2,0,1:T(8,128)(2,1)}), bf16[128,1,2048]{2,0,1:T(8,128)(2,1)}) %reduce-scatter.7.cloned.1.call-update) | async-done | bytes 524304 | tf_op jit(solution)/shard_map/reduce_scatter | solution.py:209
  450.4 15.8 %convert_bitcast_fusion.2 = bf16[2048,1,2048]{2,0,1:T(8,128)(2,1)} fusion(bf16[512,2048]{1,0:T(8,128)(2,1)S(1)} %copy-done, f32[2048,512]{1,0:T(8,128)S(1)} %copy-done.89, f32[512]{0:T(512)S(1)} %copy-done.85), kind=kOutput, calls=%fused_computation.18 | convolution fusion | flops 4309647360 | bytes 14682112 | tf_op jit(solution)/shard_map/rsf,fd->rsd/dot_general | solution.py:190
  466.2 45.6 %all-gather.11.cloned.1.call-done = bf16[2048,1,2048]{2,0,1:T(8,128)(2,1)} async-done(((bf16[128,1,2048]{2,0,1:T(8,128)(2,1)}), bf16[2048,1,2048]{2,0,1:T(8,128)(2,1)}) %all-gather.11.cloned.1.call-update) | async-done | bytes 8388624 | tf_op jit(solution)/shard_map/all_gather | solution.py:223
  511.8 5.8 fusion.45
  530.8 10.9 %multiply_reduce_fusion = (f32[512]{0:T(512)}, f32[512]{0:T(512)}, f32[512]{0:T(512)}, f32[512]{0:T(512)}, f32[512,2048]{1,0:T(8,128)}) fusion(f32[512,2048]{1,0:T(8,128)S(1)} %copy-done.2, f32[512]{0:T(512)S(1)} %copy-done.59, pred[2048]{0:T(1024)(128)(4,1)S(1)} %iota_compare_fusion.4, s32[512]{0:T(512)S(1)} %copy-done.52, f32[512,2048]{1,0:T(8,128)} %fusion.108, ...), kind=kOutput, calls=%fused_computation.31 | convolution fusion | flops 293599232 | bytes 34234368 | tf_op jit(solution)/shard_map/while/body/eval_jaxpr/dot_general | solution.py:65
  541.7 9.5 %multiply_convert_fusion = (bf16[512,2048]{1,0:T(8,128)(2,1)S(1)}, bf16[512,2048]{1,0:T(8,128)(2,1)}, bf16[512,2048]{1,0:T(8,128)(2,1)S(1)}) fusion(f32[512,2048]{1,0:T(8,128)} %get-tuple-element.119, f32[512]{0:T(512)} %get-tuple-element.82, f32[512,2048]{1,0:T(8,128)S(1)} %copy-done.2, f32[512]{0:T(512)} %get-tuple-element.124, ...), kind=kLoop, calls=%fused_computation.30 | loop fusion | flops 22020096 | bytes 31475712 | tf_op jit(solution)/shard_map/while/body/eval_jaxpr/convert_element_type | solution.py:69
  569.4 9.7 %convert_bitcast_fusion = bf16[2048,1,2048]{2,0,1:T(8,128)(2,1)} fusion(bf16[2048,384]{0,1:T(8,128)(2,1)} %bitcast.201, bf16[2048,384]{0,1:T(8,128)(2,1)} %bitcast.202), kind=kOutput, calls=%fused_computation.16 | convolution fusion | flops 3225419776 | bytes 11534336 | tf_op jit(solution)/shard_map/rsc,dc->rsd/dot_general | solution.py:250
  582.5 8.5 %fusion.27 = f32[512,2048]{1,0:T(8,128)S(1)} fusion(bf16[2048,1,2048]{2,0,1:T(8,128)(2,1)} %all-gather.7.cloned.1.call-done, f32[]{:T(128)S(6)} %div.167, f32[2048,512]{1,0:T(8,128)} %copy-done.88, f32[512]{0:T(512)S(1)} %copy-done.86), kind=kOutput, calls=%fused_computation.59 | convolution fusion | flops 4306501632 | bytes 16779268 | tf_op jit(solution)/shard_map/rsf,rsd->fd/dot_general | solution.py:194
  596.6 7.1 fusion.30
  614.4 17.2 %collective-permute-done.13 = bf16[4,256,512]{2,1,0:T(8,128)(2,1)} collective-permute-done((bf16[4,256,512]{2,1,0:T(8,128)(2,1)}, bf16[4,256,512]{2,1,0:T(8,128)(2,1)}, u32[]{:S(2)}, u32[]{:S(2)}) %collective-permute-start.13) | collective-permute-done | bytes 1048608 | tf_op jit(solution)/shard_map/ppermute | solution.py:342
  633.4 19.6 %collective-permute-done.16 = bf16[512,4,256]{2,0,1:T(8,128)(2,1)} collective-permute-done((bf16[512,4,256]{2,0,1:T(8,128)(2,1)}, bf16[512,4,256]{2,0,1:T(8,128)(2,1)}, u32[]{:S(2)}, u32[]{:S(2)}) %collective-permute-start.16) | collective-permute-done | bytes 1048608 | tf_op jit(solution)/shard_map/ppermute | solution.py:342
  661.9 5.2 collective-permute-done.15
  668.0 4.4 collective-permute-done.18
  676.4 4.7 fusion.42
  683.5 7.0 fusion.36
  709.7 26.8 %collective-permute-done.7 = bf16[4,256,3,1,128]{4,3,2,1,0:T(2,128)(2,1)} collective-permute-done((bf16[4,256,3,1,128]{4,3,2,1,0:T(2,128)(2,1)S(1)}, bf16[4,256,3,1,128]{4,3,2,1,0:T(2,128)(2,1)}, u32[]{:S(2)}, u32[]{:S(2)}) %collective-permute-start.7) | collective-permute-done | bytes 786464 | tf_op jit(solution)/shard_map/ppermute | solution.py:342
  736.5 4.7 copy_add_fusion
  755.1 7.4 collective-permute-done.9
  (371 shorter events, 160.5 us)
Async XLA Ops:
  7.2 322.2 %copy-start = (bf16[512,2048]{1,0:T(8,128)(2,1)S(1)}, bf16[512,2048]{1,0:T(8,128)(2,1)}, u32[]{:S(2)}) copy-start(bf16[512,2048]{1,0:T(8,128)(2,1)} %param.28) | copy-start | bytes 6291460
  7.2 78.3 %all-gather.5.cloned.1.call-start = ((), (), s32[]{:S(2)}) async-start(), calls=%async_computation.4 | async-start | bytes 8912896 | tf_op jit(solution)/shard_map/all_gather | solution.py:132
  12.2 146.3 %all-gather.7.cloned.1.call-start = ((), (), s32[]{:S(2)}) async-start(), calls=%async_computation.5 | async-start | bytes 8912896 | tf_op jit(solution)/shard_map/all_gather | solution.py:167
  16.8 229.8 %reduce-scatter.5.cloned.1.call-start = ((), (), s32[]{:S(2)}) async-start(), calls=%async_computation.6 | async-start | bytes 8912896 | tf_op jit(solution)/shard_map/reduce_scatter | solution.py:173
  139.4 107.3 %copy-start.9 = (bf16[128,1,2048]{2,0,1:T(8,128)(2,1)S(1)}, bf16[128,1,2048]{2,0,1:T(8,128)(2,1)}, u32[]{:S(2)}) copy-start(bf16[128,1,2048]{2,0,1:T(8,128)(2,1)} %param.15) | copy-start | bytes 1572868
  139.4 107.3 %copy-start.39 = (f32[2048]{0:T(1024)S(1)}, f32[2048]{0:T(1024)}, u32[]{:S(2)}) copy-start(f32[2048]{0:T(1024)} %param.23) | copy-start | bytes 24580
  139.4 110.0 %copy-start.47 = (f32[2048]{0:T(1024)S(1)}, f32[2048]{0:T(1024)}, u32[]{:S(2)}) copy-start(f32[2048]{0:T(1024)} %param.24) | copy-start | bytes 24580
  139.4 110.0 %copy-start.70 = (f32[2048]{0:T(1024)S(1)}, f32[2048]{0:T(1024)}, u32[]{:S(2)}) copy-start(f32[2048]{0:T(1024)} %param.25) | copy-start | bytes 24580
  158.6 163.3 %all-gather.9.cloned.1.call-start = ((), (), s32[]{:S(2)}) async-start(), calls=%async_computation.7 | async-start | bytes 8912896 | tf_op jit(solution)/shard_map/all_gather | solution.py:180
  251.6 184.1 %reduce-scatter.7.cloned.1.call-start = ((), (), s32[]{:S(2)}) async-start(), calls=%async_computation.8 | async-start | bytes 8912896 | tf_op jit(solution)/shard_map/reduce_scatter | solution.py:209
  350.9 160.9 %all-gather.11.cloned.1.call-start = ((), (), s32[]{:S(2)}) async-start(), calls=%async_computation.9 | async-start | bytes 8912896 | tf_op jit(solution)/shard_map/all_gather | solution.py:223
  441.6 260.6 %reduce-scatter.11.cloned.1.call-start = ((), (), s32[]{:S(2)}) async-start(), calls=%async_computation.11 | async-start | bytes 8912896 | tf_op jit(solution)/shard_map/reduce_scatter | solution.py:249
  579.1 186.7 %reduce-scatter.9.cloned.1.call-start = ((), (), s32[]{:S(2)}) async-start(), calls=%async_computation.10 | async-start | bytes 8912896 | tf_op jit(solution)/shard_map/reduce_scatter | solution.py:226
  605.1 26.5 %collective-permute-start.13 = (bf16[4,256,512]{2,1,0:T(8,128)(2,1)}, bf16[4,256,512]{2,1,0:T(8,128)(2,1)}, u32[]{:S(2)}, u32[]{:S(2)}) collective-permute-start(bf16[4,256,512]{2,1,0:T(8,128)(2,1)} %bitcast.57), channel_id=1, source_target_pairs={{0,64},{32,96},{64,0},{96,32},{1,65},{33,97},{65,1},{97,33},{2,66}... | collective-permute-start | bytes 3145736 | tf_op jit(solution)/shard_map/ppermute | solution.py:342
  610.4 42.5 %collective-permute-start.16 = (bf16[512,4,256]{2,0,1:T(8,128)(2,1)}, bf16[512,4,256]{2,0,1:T(8,128)(2,1)}, u32[]{:S(2)}, u32[]{:S(2)}) collective-permute-start(bf16[512,4,256]{2,0,1:T(8,128)(2,1)} %select_convert_fusion), channel_id=1, source_target_pairs={{0,64},{32,96},{64,0},{96,32},{1,65},{33,97},{65,1},{97,33},{2,66}... | collective-permute-start | bytes 3145736 | tf_op jit(solution)/shard_map/ppermute | solution.py:342
  633.3 21.9 %collective-permute-start.14 = (bf16[2,256,512]{2,1,0:T(8,128)(2,1)S(1)}, bf16[2,256,512]{2,1,0:T(8,128)(2,1)S(1)}, u32[]{:S(2)}, u32[]{:S(2)}) collective-permute-start(bf16[2,256,512]{2,1,0:T(8,128)(2,1)S(1)} %select_convert_fusion.4), channel_id=1, source_target_pairs={{0,32},{32,0},{64,96},{96,64},{1,33},{33,1},{65,97},{97,65},{2,34}... | collective-permute-start | bytes 1572872 | tf_op jit(solution)/shard_map/ppermute | solution.py:342
  655.0 4.4 collective-permute-start.17
  656.2 10.9 %collective-permute-start.15 = (bf16[1,256,512]{2,1,0:T(8,128)(2,1)}, bf16[1,256,512]{2,1,0:T(8,128)(2,1)S(1)}, u32[]{:S(2)}, u32[]{:S(2)}) collective-permute-start(bf16[1,256,512]{2,1,0:T(8,128)(2,1)} %select_convert_fusion.6), channel_id=1, source_target_pairs={{0,16},{16,0},{1,17},{17,1},{2,18},{18,2},{3,19},{19,3},{4,20},{20... | collective-permute-start | bytes 786440 | tf_op jit(solution)/shard_map/ppermute | solution.py:342
  660.4 12.0 %collective-permute-start.18 = (bf16[512,1,256]{2,0,1:T(8,128)(2,1)}, bf16[512,1,256]{2,0,1:T(8,128)(2,1)}, u32[]{:S(2)}, u32[]{:S(2)}) collective-permute-start(bf16[512,1,256]{2,0,1:T(8,128)(2,1)} %select_convert_fusion.5), channel_id=1, source_target_pairs={{0,16},{16,0},{1,17},{17,1},{2,18},{18,2},{3,19},{19,3},{4,20},{20... | collective-permute-start | bytes 786440 | tf_op jit(solution)/shard_map/ppermute | solution.py:342
  681.8 10.1 %collective-permute-start.10 = (bf16[1,128,4,256]{3,1,2,0:T(8,128)(2,1)S(1)}, bf16[1,128,4,256]{3,1,2,0:T(8,128)(2,1)S(1)}, u32[]{:S(2)}, u32[]{:S(2)}) collective-permute-start(bf16[1,128,4,256]{3,1,2,0:T(8,128)(2,1)S(1)} %select_convert_fusion.7), channel_id=1, source_target_pairs={{0,64},{32,96},{64,0},{96,32},{1,65},{33,97},{65,1},{97,33},{2,66}... | collective-permute-start | bytes 786440 | tf_op jit(solution)/shard_map/ppermute | solution.py:342
  692.2 1.4 collective-permute-start.11
  694.4 6.3 collective-permute-start.12
  700.2 36.4 %collective-permute-start.7 = (bf16[4,256,3,1,128]{4,3,2,1,0:T(2,128)(2,1)S(1)}, bf16[4,256,3,1,128]{4,3,2,1,0:T(2,128)(2,1)}, u32[]{:S(2)}, u32[]{:S(2)}) collective-permute-start(bf16[4,256,3,1,128]{4,3,2,1,0:T(2,128)(2,1)S(1)} %copy.55), channel_id=1, source_target_pairs={{0,64},{32,96},{64,0},{96,32},{1,65},{33,97},{65,1},{97,33},{2,66}... | collective-permute-start | bytes 2359304 | tf_op jit(solution)/shard_map/ppermute | solution.py:342
  706.6 34.6 %collective-permute-start = (f32[8,8,192]{2,0,1:T(8,128)S(1)}, f32[8,8,192]{2,0,1:T(8,128)S(1)}, u32[]{:S(2)}, u32[]{:S(2)}) collective-permute-start(f32[8,8,192]{2,0,1:T(8,128)S(1)} %slice_select_fusion.2), channel_id=1, source_target_pairs={{0,8},{1,9},{2,10},{3,11},{4,12},{5,13},{6,14},{7,15},{8,0},{9,1},... | collective-permute-start | bytes 147464 | tf_op jit(solution)/shard_map/ppermute | solution.py:342
  741.3 4.5 collective-permute-start.1
  743.6 5.4 collective-permute-start.8
  745.9 5.4 collective-permute-start.2
  751.3 3.7 collective-permute-start.3
  753.2 9.4 %collective-permute-start.9 = (bf16[1,256,3,1,128]{4,3,2,1,0:T(2,128)(2,1)S(1)}, bf16[1,256,3,1,128]{4,3,2,1,0:T(2,128)(2,1)S(1)}, u32[]{:S(2)}, u32[]{:S(2)}) collective-permute-start(bf16[1,256,3,1,128]{4,3,2,1,0:T(2,128)(2,1)S(1)} %fusion.96), channel_id=1, source_target_pairs={{0,16},{16,0},{1,17},{17,1},{2,18},{18,2},{3,19},{19,3},{4,20},{20... | collective-permute-start | bytes 589832 | tf_op jit(solution)/shard_map/ppermute | solution.py:342
  755.1 9.0 %collective-permute-start.4 = (f32[1,4,192]{2,0,1:T(1,128)S(1)}, f32[1,4,192]{2,0,1:T(1,128)S(1)}, u32[]{:S(2)}, u32[]{:S(2)}) collective-permute-start(f32[1,4,192]{2,0,1:T(1,128)S(1)} %broadcast_select_fusion.8), channel_id=1, source_target_pairs={{0,64},{32,96},{64,0},{96,32},{1,65},{33,97},{65,1},{97,33},{2,66}... | collective-permute-start | bytes 9224 | tf_op jit(solution)/shard_map/ppermute | solution.py:342
  764.0 1.2 collective-permute-start.5
  765.3 5.2 collective-permute-start.6
  (87 other events, 1435.8 us)
Sparse Core Ops, SparseCore 0:
  12.4 73.0 all-gather.4
  88.2 70.3 all-gather.6
  162.0 84.6 reduce-scatter.4
  251.8 70.0 all-gather.8
  351.0 84.6 reduce-scatter.6
  441.7 70.0 all-gather.10
  579.2 84.8 reduce-scatter.10
  667.6 85.7 reduce-scatter.8
where the time goes:
time: 789 us; the launch traced here: 779 us
  waiting for transfers between devices  461 us (58%)
  matrix products  155 us (20%)
  other arithmetic  78.1 us (10%)
  local copies, waits for them, and re-layouts  28.2 us (4%)
  starting transfers between devices  22.8 us (3%)
  between operations  17.3 us (2%)
  Pallas kernels  16.6 us (2%)
    ppermute x19, waiting for transfers between devices, halving_steps(): got = lax.ppermute(send, axis, [(i, i ^ bit) for i in range(size)])  88.2 us
    reduce_scatter x1, waiting for transfers between devices, shards(): lax.psum_scatter(attention_part, 'tensor', scatter_dimension=0, tiled=True)  88.1 us
    reduce_scatter x1, waiting for transfers between devices, shards(): lax.psum_scatter(jnp.einsum('rsf,df->rsd', piece, w_in, preferred_element...  84.8 us
    all_gather x1, waiting for transfers between devices, shards(): second_full = lax.all_gather(second_low, 'tensor', axis=0, tiled=True)  70.2 us
    all_gather x1, waiting for transfers between devices, shards(): normed_full = lax.all_gather(normed_low, 'tensor', axis=0, tiled=True)  65.2 us
    all_gather x1, waiting for transfers between devices, shards(): piece = lax.all_gather(branch_low, 'tensor', axis=0, tiled=True)  45.6 us
    ppermute x19, starting transfers between devices, halving_steps(): got = lax.ppermute(send, axis, [(i, i ^ bit) for i in range(size)])  22.5 us
    dot_general x4, matrix products, attend_backward(): lax.dot_general(grad_rows, value_rows, (((1,), (1,)), ((), ())), preferre...  21.5 us
  transfers between devices with their start and end apart: 27, of which 19 were waited for; matrix products, arithmetic and copies ran while one was open for 18% of the time, Pallas kernels for 2%

commit v1 on v0

--- a/solution.py
+++ b/solution.py
@@ -177,7 +177,14 @@
     )
     middle = inputs + attention
     second_low = layer_norm(middle, ln2_gain, ln2_bias).astype(jnp.bfloat16)
-    second_full = lax.all_gather(second_low, "tensor", axis=0, tiled=True)
+    ring = [second_low]
+    for hop in range(15):
+        ring.append(lax.ppermute(ring[-1], "tensor", [(dev, (dev + 1) % 16) for dev in range(16)]))
+    second_full = jnp.roll(
+        jnp.concatenate(ring[::-1], axis=0),
+        (lax.axis_index("tensor") + 1) * ring[0].shape[0],
+        axis=0,
+    )
     pre_act = (
         jnp.dot(
             second_full.reshape(seq_total * seq_count, model_width),

time: 789 us -> 951 us (1.21)
  waiting for transfers between devices: 461 us -> 609 us
  local copies, waits for them, and re-layouts: 28.2 us -> 58 us
  matrix products: 155 us -> 138 us
    ppermute x0 -> x15, waiting for transfers between devices: none -> 222 us  [shards(): lax.ppermute(ring[-1], 'tensor', [(dev, (dev + 1) % 16) for dev in range(...]
    all_gather x1 -> x0, waiting for transfers between devices: 70.2 us -> none  [shards(): second_full = lax.all_gather(second_low, 'tensor', axis=0, tiled=True)]
    unnamed x187 -> x278, local copies, waits for them, and re-layouts: 15.3 us -> 41.4 us
  transfers between devices with their start and end apart: 27 -> 41, of which waited for: 19 -> 33; matrix products, arithmetic and copies ran while one was open for 18% -> 15% of each run, Pallas kernels for 2% -> 2%
where the time goes in v1:
time: 951 us; the launch traced here: 941 us
  waiting for transfers between devices  609 us (64%)
  matrix products  138 us (15%)
  other arithmetic  78.7 us (8%)
  local copies, waits for them, and re-layouts  58 us (6%)
  starting transfers between devices  24 us (3%)
  between operations  17.8 us (2%)
  Pallas kernels  16.6 us (2%)
    ppermute x15, waiting for transfers between devices, shards(): lax.ppermute(ring[-1], 'tensor', [(dev, (dev + 1) % 16) for dev in range(...  222 us
    reduce_scatter x1, waiting for transfers between devices, shards(): lax.psum_scatter(attention_part, 'tensor', scatter_dimension=0, tiled=True)  88.1 us
    reduce_scatter x1, waiting for transfers between devices, shards(): lax.psum_scatter(jnp.einsum('rsf,df->rsd', piece, w_in, preferred_element...  81.3 us
    ppermute x19, waiting for transfers between devices, halving_steps(): got = lax.ppermute(send, axis, [(i, i ^ bit) for i in range(size)])  80 us
    all_gather x1, waiting for transfers between devices, shards(): normed_full = lax.all_gather(normed_low, 'tensor', axis=0, tiled=True)  65.2 us
    all_gather x1, waiting for transfers between devices, shards(): piece = lax.all_gather(branch_low, 'tensor', axis=0, tiled=True)  53.2 us
    unnamed x278, local copies, waits for them, and re-layouts  41.4 us
    ppermute x19, starting transfers between devices, halving_steps(): got = lax.ppermute(send, axis, [(i, i ^ bit) for i in range(size)])  22.1 us
  transfers between devices with their start and end apart: 41, of which 33 were waited for; matrix products, arithmetic and copies ran while one was open for 15% of the time, Pallas kernels for 2%

profile of v1, /device:TPU:0, one launch (start us, length us, event | category | flops | bytes accessed | tf_op | source)
XLA Modules:
  0.0 941.5 jit_solution(2740104426344165628)
XLA Ops:
  20.3 65.2 %all-gather.4.cloned.1.call-done = bf16[2048,1,2048]{2,0,1:T(8,128)(2,1)} async-done(((bf16[128,1,2048]{2,0,1:T(8,128)(2,1)}), bf16[2048,1,2048]{2,0,1:T(8,128)(2,1)}) %all-gather.4.cloned.1.call-update) | async-done | bytes 8388624 | tf_op jit(solution)/shard_map/all_gather | solution.py:132
  85.5 7.4 fusion.35
  139.7 18.3 %all-gather.6.cloned.1.call-done = bf16[2048,1,2048]{2,0,1:T(8,128)(2,1)} async-done(((bf16[128,1,2048]{2,0,1:T(8,128)(2,1)}), bf16[2048,1,2048]{2,0,1:T(8,128)(2,1)}) %all-gather.6.cloned.1.call-update) | async-done | bytes 8388624 | tf_op jit(solution)/shard_map/all_gather | solution.py:167
  158.0 88.1 %reduce-scatter.5.cloned.1.call-done = bf16[128,1,2048]{2,0,1:T(8,128)(2,1)} async-done(((bf16[2048,1,2048]{2,0,1:T(8,128)(2,1)}), bf16[128,1,2048]{2,0,1:T(8,128)(2,1)}) %reduce-scatter.5.cloned.1.call-update) | async-done | bytes 524304 | tf_op jit(solution)/shard_map/reduce_scatter | solution.py:173
  251.8 14.3 %collective-permute-done = bf16[128,1,2048]{2,0,1:T(8,128)(2,1)S(1)} collective-permute-done((bf16[128,1,2048]{2,0,1:T(8,128)(2,1)S(1)}, bf16[128,1,2048]{2,0,1:T(8,128)(2,1)S(1)}, u32[]{:S(2)}, u32[]{:S(2)}) %collective-permute-start) | collective-permute-done | bytes 524320 | tf_op jit(solution)/shard_map/ppermute | solution.py:182
  267.0 14.9 %collective-permute-done.1 = bf16[128,1,2048]{2,0,1:T(8,128)(2,1)S(1)} collective-permute-done((bf16[128,1,2048]{2,0,1:T(8,128)(2,1)S(1)}, bf16[128,1,2048]{2,0,1:T(8,128)(2,1)S(1)}, u32[]{:S(2)}, u32[]{:S(2)}) %collective-permute-start.1) | collective-permute-done | bytes 524320 | tf_op jit(solution)/shard_map/ppermute | solution.py:182
  282.7 14.0 %collective-permute-done.2 = bf16[128,1,2048]{2,0,1:T(8,128)(2,1)S(1)} collective-permute-done((bf16[128,1,2048]{2,0,1:T(8,128)(2,1)S(1)}, bf16[128,1,2048]{2,0,1:T(8,128)(2,1)S(1)}, u32[]{:S(2)}, u32[]{:S(2)}) %collective-permute-start.2) | collective-permute-done | bytes 524320 | tf_op jit(solution)/shard_map/ppermute | solution.py:182
  297.5 13.0 %collective-permute-done.3 = bf16[128,1,2048]{2,0,1:T(8,128)(2,1)S(1)} collective-permute-done((bf16[128,1,2048]{2,0,1:T(8,128)(2,1)S(1)}, bf16[128,1,2048]{2,0,1:T(8,128)(2,1)S(1)}, u32[]{:S(2)}, u32[]{:S(2)}) %collective-permute-start.3) | collective-permute-done | bytes 524320 | tf_op jit(solution)/shard_map/ppermute | solution.py:182
  311.3 12.5 %collective-permute-done.4 = bf16[128,1,2048]{2,0,1:T(8,128)(2,1)S(1)} collective-permute-done((bf16[128,1,2048]{2,0,1:T(8,128)(2,1)S(1)}, bf16[128,1,2048]{2,0,1:T(8,128)(2,1)S(1)}, u32[]{:S(2)}, u32[]{:S(2)}) %collective-permute-start.4) | collective-permute-done | bytes 524320 | tf_op jit(solution)/shard_map/ppermute | solution.py:182
  324.6 13.0 %collective-permute-done.5 = bf16[128,1,2048]{2,0,1:T(8,128)(2,1)S(1)} collective-permute-done((bf16[128,1,2048]{2,0,1:T(8,128)(2,1)S(1)}, bf16[128,1,2048]{2,0,1:T(8,128)(2,1)S(1)}, u32[]{:S(2)}, u32[]{:S(2)}) %collective-permute-start.5) | collective-permute-done | bytes 524320 | tf_op jit(solution)/shard_map/ppermute | solution.py:182
  338.5 14.1 %collective-permute-done.6 = bf16[128,1,2048]{2,0,1:T(8,128)(2,1)S(1)} collective-permute-done((bf16[128,1,2048]{2,0,1:T(8,128)(2,1)S(1)}, bf16[128,1,2048]{2,0,1:T(8,128)(2,1)S(1)}, u32[]{:S(2)}, u32[]{:S(2)}) %collective-permute-start.6) | collective-permute-done | bytes 524320 | tf_op jit(solution)/shard_map/ppermute | solution.py:182
  353.4 15.2 %collective-permute-done.7 = bf16[128,1,2048]{2,0,1:T(8,128)(2,1)S(1)} collective-permute-done((bf16[128,1,2048]{2,0,1:T(8,128)(2,1)S(1)}, bf16[128,1,2048]{2,0,1:T(8,128)(2,1)S(1)}, u32[]{:S(2)}, u32[]{:S(2)}) %collective-permute-start.7) | collective-permute-done | bytes 524320 | tf_op jit(solution)/shard_map/ppermute | solution.py:182
  369.4 16.3 %collective-permute-done.8 = bf16[128,1,2048]{2,0,1:T(8,128)(2,1)S(1)} collective-permute-done((bf16[128,1,2048]{2,0,1:T(8,128)(2,1)S(1)}, bf16[128,1,2048]{2,0,1:T(8,128)(2,1)S(1)}, u32[]{:S(2)}, u32[]{:S(2)}) %collective-permute-start.8) | collective-permute-done | bytes 524320 | tf_op jit(solution)/shard_map/ppermute | solution.py:182
  386.5 17.5 %collective-permute-done.9 = bf16[128,1,2048]{2,0,1:T(8,128)(2,1)S(1)} collective-permute-done((bf16[128,1,2048]{2,0,1:T(8,128)(2,1)S(1)}, bf16[128,1,2048]{2,0,1:T(8,128)(2,1)S(1)}, u32[]{:S(2)}, u32[]{:S(2)}) %collective-permute-start.9) | collective-permute-done | bytes 524320 | tf_op jit(solution)/shard_map/ppermute | solution.py:182
  404.8 17.6 %collective-permute-done.10 = bf16[128,1,2048]{2,0,1:T(8,128)(2,1)S(1)} collective-permute-done((bf16[128,1,2048]{2,0,1:T(8,128)(2,1)S(1)}, bf16[128,1,2048]{2,0,1:T(8,128)(2,1)S(1)}, u32[]{:S(2)}, u32[]{:S(2)}) %collective-permute-start.10) | collective-permute-done | bytes 524320 | tf_op jit(solution)/shard_map/ppermute | solution.py:182
  423.2 16.8 %collective-permute-done.11 = bf16[128,1,2048]{2,0,1:T(8,128)(2,1)S(1)} collective-permute-done((bf16[128,1,2048]{2,0,1:T(8,128)(2,1)S(1)}, bf16[128,1,2048]{2,0,1:T(8,128)(2,1)S(1)}, u32[]{:S(2)}, u32[]{:S(2)}) %collective-permute-start.11) | collective-permute-done | bytes 524320 | tf_op jit(solution)/shard_map/ppermute | solution.py:182
  440.8 15.9 %collective-permute-done.12 = bf16[128,1,2048]{2,0,1:T(8,128)(2,1)S(1)} collective-permute-done((bf16[128,1,2048]{2,0,1:T(8,128)(2,1)S(1)}, bf16[128,1,2048]{2,0,1:T(8,128)(2,1)S(1)}, u32[]{:S(2)}, u32[]{:S(2)}) %collective-permute-start.12) | collective-permute-done | bytes 524320 | tf_op jit(solution)/shard_map/ppermute | solution.py:182
  457.5 14.5 %collective-permute-done.13 = bf16[128,1,2048]{2,0,1:T(8,128)(2,1)} collective-permute-done((bf16[128,1,2048]{2,0,1:T(8,128)(2,1)S(1)}, bf16[128,1,2048]{2,0,1:T(8,128)(2,1)}, u32[]{:S(2)}, u32[]{:S(2)}) %collective-permute-start.13) | collective-permute-done | bytes 524320 | tf_op jit(solution)/shard_map/ppermute | solution.py:182
  472.0 12.8 %collective-permute-done.14 = bf16[128,1,2048]{2,0,1:T(8,128)(2,1)} collective-permute-done((bf16[128,1,2048]{2,0,1:T(8,128)(2,1)}, bf16[128,1,2048]{2,0,1:T(8,128)(2,1)}, u32[]{:S(2)}, u32[]{:S(2)}) %collective-permute-start.14) | collective-permute-done | bytes 524320 | tf_op jit(solution)/shard_map/ppermute | solution.py:182
  493.7 7.4 copy-done.93
  507.5 9.9 %convert_reduce_fusion = (f32[512]{0:T(512)}, bf16[2048,512]{1,0:T(8,128)(2,1)S(1)}) fusion(f32[2048,512]{1,0:T(8,128)} %fusion.10, f32[512]{0:T(512)S(1)} %copy-done.115, bf16[512,2048]{1,0:T(8,128)(2,1)S(1)} %copy-done, bf16[2048,1,2048]{2,0,1:T(8,128)(2,1)S(1)} %bitcast.213), kind=kOutput, calls=%fused_computation.31 | convolution fusion | flops 4319084032 | bytes 16781312 | tf_op jit(solution)/shard_map/rsd,fd->rsf/dot_general | solution.py:202
  525.6 81.3 %reduce-scatter.7.cloned.1.call-done = bf16[128,1,2048]{2,0,1:T(8,128)(2,1)} async-done(((bf16[2048,1,2048]{2,0,1:T(8,128)(2,1)}), bf16[128,1,2048]{2,0,1:T(8,128)(2,1)}) %reduce-scatter.7.cloned.1.call-update) | async-done | bytes 524304 | tf_op jit(solution)/shard_map/reduce_scatter | solution.py:216
  629.7 53.2 %all-gather.8.cloned.1.call-done = bf16[2048,1,2048]{2,0,1:T(8,128)(2,1)} async-done(((bf16[128,1,2048]{2,0,1:T(8,128)(2,1)}), bf16[2048,1,2048]{2,0,1:T(8,128)(2,1)}) %all-gather.8.cloned.1.call-update) | async-done | bytes 8388624 | tf_op jit(solution)/shard_map/all_gather | solution.py:230
  697.9 10.1 %multiply_reduce_fusion = (f32[512]{0:T(512)}, f32[512]{0:T(512)}, f32[512]{0:T(512)}, f32[512]{0:T(512)}, f32[512,2048]{1,0:T(8,128)}) fusion(f32[512,2048]{1,0:T(8,128)S(1)} %copy-done.4, f32[512]{0:T(512)S(1)} %copy-done.87, pred[2048]{0:T(1024)(128)(4,1)S(1)} %iota_compare_fusion.4, s32[512]{0:T(512)S(1)} %iota_add_fusion, f32[512,2048]{1,0:T(8,128)} %fusion.110, ...), kind=kOutput, calls=%fused_computation.33 | convolution fusion | flops 293599232 | bytes 34234368 | tf_op jit(solution)/shard_map/while/body/eval_jaxpr/dot_general | solution.py:65
  708.0 9.3 multiply_convert_fusion
  736.3 9.7 %convert_bitcast_fusion = bf16[2048,1,2048]{2,0,1:T(8,128)(2,1)} fusion(bf16[2048,384]{0,1:T(8,128)(2,1)} %bitcast.202, bf16[2048,384]{0,1:T(8,128)(2,1)} %bitcast.201), kind=kOutput, calls=%fused_computation.16 | convolution fusion | flops 3225419776 | bytes 11534336 | tf_op jit(solution)/shard_map/rsc,dc->rsd/dot_general | solution.py:257
  749.5 8.5 fusion.29
  769.6 7.4 fusion.32
  784.1 10.3 %collective-permute-done.31 = bf16[512,4,256]{2,0,1:T(8,128)(2,1)} collective-permute-done((bf16[512,4,256]{2,0,1:T(8,128)(2,1)}, bf16[512,4,256]{2,0,1:T(8,128)(2,1)}, u32[]{:S(2)}, u32[]{:S(2)}) %collective-permute-start.31) | collective-permute-done | bytes 1048608 | tf_op jit(solution)/shard_map/ppermute | solution.py:349
  796.5 19.2 %collective-permute-done.28 = bf16[4,256,512]{2,1,0:T(8,128)(2,1)} collective-permute-done((bf16[4,256,512]{2,1,0:T(8,128)(2,1)}, bf16[4,256,512]{2,1,0:T(8,128)(2,1)}, u32[]{:S(2)}, u32[]{:S(2)}) %collective-permute-start.28) | collective-permute-done | bytes 1048608 | tf_op jit(solution)/shard_map/ppermute | solution.py:349
  872.3 26.7 %collective-permute-done.22 = bf16[4,256,3,1,128]{4,3,2,1,0:T(2,128)(2,1)} collective-permute-done((bf16[4,256,3,1,128]{4,3,2,1,0:T(2,128)(2,1)S(1)}, bf16[4,256,3,1,128]{4,3,2,1,0:T(2,128)(2,1)}, u32[]{:S(2)}, u32[]{:S(2)}) %collective-permute-start.22) | collective-permute-done | bytes 786464 | tf_op jit(solution)/shard_map/ppermute | solution.py:349
  917.2 7.5 collective-permute-done.24
  (491 shorter events, 261.9 us)
Async XLA Ops:
  7.2 78.3 %all-gather.4.cloned.1.call-start = ((), (), s32[]{:S(2)}) async-start(), calls=%async_computation.4 | async-start | bytes 8912896 | tf_op jit(solution)/shard_map/all_gather | solution.py:132
  12.2 145.7 %all-gather.6.cloned.1.call-start = ((), (), s32[]{:S(2)}) async-start(), calls=%async_computation.5 | async-start | bytes 8912896 | tf_op jit(solution)/shard_map/all_gather | solution.py:167
  16.8 229.3 %reduce-scatter.5.cloned.1.call-start = ((), (), s32[]{:S(2)}) async-start(), calls=%async_computation.6 | async-start | bytes 8912896 | tf_op jit(solution)/shard_map/reduce_scatter | solution.py:173
  158.0 448.8 %reduce-scatter.7.cloned.1.call-start = ((), (), s32[]{:S(2)}) async-start(), calls=%async_computation.7 | async-start | bytes 8912896 | tf_op jit(solution)/shard_map/reduce_scatter | solution.py:216
  250.2 15.9 %collective-permute-start = (bf16[128,1,2048]{2,0,1:T(8,128)(2,1)S(1)}, bf16[128,1,2048]{2,0,1:T(8,128)(2,1)S(1)}, u32[]{:S(2)}, u32[]{:S(2)}) collective-permute-start(bf16[128,1,2048]{2,0,1:T(8,128)(2,1)S(1)} %add_convert_fusion.3), channel_id=1, source_target_pairs={{0,1},{1,2},{2,3},{3,4},{4,5},{5,6},{6,7},{7,8},{8,9},{9,10},{10,1... | collective-permute-start | bytes 1572872 | tf_op jit(solution)/shard_map/ppermute | solution.py:182
  267.0 14.9 %collective-permute-start.1 = (bf16[128,1,2048]{2,0,1:T(8,128)(2,1)S(1)}, bf16[128,1,2048]{2,0,1:T(8,128)(2,1)S(1)}, u32[]{:S(2)}, u32[]{:S(2)}) collective-permute-start(bf16[128,1,2048]{2,0,1:T(8,128)(2,1)S(1)} %collective-permute-done), channel_id=1, source_target_pairs={{0,1},{1,2},{2,3},{3,4},{4,5},{5,6},{6,7},{7,8},{8,9},{9,10},{10,1... | collective-permute-start | bytes 1572872 | tf_op jit(solution)/shard_map/ppermute | solution.py:182
  282.7 14.0 %collective-permute-start.2 = (bf16[128,1,2048]{2,0,1:T(8,128)(2,1)S(1)}, bf16[128,1,2048]{2,0,1:T(8,128)(2,1)S(1)}, u32[]{:S(2)}, u32[]{:S(2)}) collective-permute-start(bf16[128,1,2048]{2,0,1:T(8,128)(2,1)S(1)} %collective-permute-done.1), channel_id=1, source_target_pairs={{0,1},{1,2},{2,3},{3,4},{4,5},{5,6},{6,7},{7,8},{8,9},{9,10},{10,1... | collective-permute-start | bytes 1572872 | tf_op jit(solution)/shard_map/ppermute | solution.py:182
  297.5 13.0 %collective-permute-start.3 = (bf16[128,1,2048]{2,0,1:T(8,128)(2,1)S(1)}, bf16[128,1,2048]{2,0,1:T(8,128)(2,1)S(1)}, u32[]{:S(2)}, u32[]{:S(2)}) collective-permute-start(bf16[128,1,2048]{2,0,1:T(8,128)(2,1)S(1)} %collective-permute-done.2), channel_id=1, source_target_pairs={{0,1},{1,2},{2,3},{3,4},{4,5},{5,6},{6,7},{7,8},{8,9},{9,10},{10,1... | collective-permute-start | bytes 1572872 | tf_op jit(solution)/shard_map/ppermute | solution.py:182
  311.3 12.5 %collective-permute-start.4 = (bf16[128,1,2048]{2,0,1:T(8,128)(2,1)S(1)}, bf16[128,1,2048]{2,0,1:T(8,128)(2,1)S(1)}, u32[]{:S(2)}, u32[]{:S(2)}) collective-permute-start(bf16[128,1,2048]{2,0,1:T(8,128)(2,1)S(1)} %collective-permute-done.3), channel_id=1, source_target_pairs={{0,1},{1,2},{2,3},{3,4},{4,5},{5,6},{6,7},{7,8},{8,9},{9,10},{10,1... | collective-permute-start | bytes 1572872 | tf_op jit(solution)/shard_map/ppermute | solution.py:182
  324.6 13.0 %collective-permute-start.5 = (bf16[128,1,2048]{2,0,1:T(8,128)(2,1)S(1)}, bf16[128,1,2048]{2,0,1:T(8,128)(2,1)S(1)}, u32[]{:S(2)}, u32[]{:S(2)}) collective-permute-start(bf16[128,1,2048]{2,0,1:T(8,128)(2,1)S(1)} %collective-permute-done.4), channel_id=1, source_target_pairs={{0,1},{1,2},{2,3},{3,4},{4,5},{5,6},{6,7},{7,8},{8,9},{9,10},{10,1... | collective-permute-start | bytes 1572872 | tf_op jit(solution)/shard_map/ppermute | solution.py:182
  338.5 14.1 %collective-permute-start.6 = (bf16[128,1,2048]{2,0,1:T(8,128)(2,1)S(1)}, bf16[128,1,2048]{2,0,1:T(8,128)(2,1)S(1)}, u32[]{:S(2)}, u32[]{:S(2)}) collective-permute-start(bf16[128,1,2048]{2,0,1:T(8,128)(2,1)S(1)} %collective-permute-done.5), channel_id=1, source_target_pairs={{0,1},{1,2},{2,3},{3,4},{4,5},{5,6},{6,7},{7,8},{8,9},{9,10},{10,1... | collective-permute-start | bytes 1572872 | tf_op jit(solution)/shard_map/ppermute | solution.py:182
  353.4 15.2 %collective-permute-start.7 = (bf16[128,1,2048]{2,0,1:T(8,128)(2,1)S(1)}, bf16[128,1,2048]{2,0,1:T(8,128)(2,1)S(1)}, u32[]{:S(2)}, u32[]{:S(2)}) collective-permute-start(bf16[128,1,2048]{2,0,1:T(8,128)(2,1)S(1)} %collective-permute-done.6), channel_id=1, source_target_pairs={{0,1},{1,2},{2,3},{3,4},{4,5},{5,6},{6,7},{7,8},{8,9},{9,10},{10,1... | collective-permute-start | bytes 1572872 | tf_op jit(solution)/shard_map/ppermute | solution.py:182
  369.4 16.3 %collective-permute-start.8 = (bf16[128,1,2048]{2,0,1:T(8,128)(2,1)S(1)}, bf16[128,1,2048]{2,0,1:T(8,128)(2,1)S(1)}, u32[]{:S(2)}, u32[]{:S(2)}) collective-permute-start(bf16[128,1,2048]{2,0,1:T(8,128)(2,1)S(1)} %collective-permute-done.7), channel_id=1, source_target_pairs={{0,1},{1,2},{2,3},{3,4},{4,5},{5,6},{6,7},{7,8},{8,9},{9,10},{10,1... | collective-permute-start | bytes 1572872 | tf_op jit(solution)/shard_map/ppermute | solution.py:182
  386.5 17.5 %collective-permute-start.9 = (bf16[128,1,2048]{2,0,1:T(8,128)(2,1)S(1)}, bf16[128,1,2048]{2,0,1:T(8,128)(2,1)S(1)}, u32[]{:S(2)}, u32[]{:S(2)}) collective-permute-start(bf16[128,1,2048]{2,0,1:T(8,128)(2,1)S(1)} %collective-permute-done.8), channel_id=1, source_target_pairs={{0,1},{1,2},{2,3},{3,4},{4,5},{5,6},{6,7},{7,8},{8,9},{9,10},{10,1... | collective-permute-start | bytes 1572872 | tf_op jit(solution)/shard_map/ppermute | solution.py:182
  404.8 17.6 %collective-permute-start.10 = (bf16[128,1,2048]{2,0,1:T(8,128)(2,1)S(1)}, bf16[128,1,2048]{2,0,1:T(8,128)(2,1)S(1)}, u32[]{:S(2)}, u32[]{:S(2)}) collective-permute-start(bf16[128,1,2048]{2,0,1:T(8,128)(2,1)S(1)} %collective-permute-done.9), channel_id=1, source_target_pairs={{0,1},{1,2},{2,3},{3,4},{4,5},{5,6},{6,7},{7,8},{8,9},{9,10},{10,1... | collective-permute-start | bytes 1572872 | tf_op jit(solution)/shard_map/ppermute | solution.py:182
  423.2 16.8 %collective-permute-start.11 = (bf16[128,1,2048]{2,0,1:T(8,128)(2,1)S(1)}, bf16[128,1,2048]{2,0,1:T(8,128)(2,1)S(1)}, u32[]{:S(2)}, u32[]{:S(2)}) collective-permute-start(bf16[128,1,2048]{2,0,1:T(8,128)(2,1)S(1)} %collective-permute-done.10), channel_id=1, source_target_pairs={{0,1},{1,2},{2,3},{3,4},{4,5},{5,6},{6,7},{7,8},{8,9},{9,10},{10,1... | collective-permute-start | bytes 1572872 | tf_op jit(solution)/shard_map/ppermute | solution.py:182
  440.8 15.9 %collective-permute-start.12 = (bf16[128,1,2048]{2,0,1:T(8,128)(2,1)S(1)}, bf16[128,1,2048]{2,0,1:T(8,128)(2,1)S(1)}, u32[]{:S(2)}, u32[]{:S(2)}) collective-permute-start(bf16[128,1,2048]{2,0,1:T(8,128)(2,1)S(1)} %collective-permute-done.11), channel_id=1, source_target_pairs={{0,1},{1,2},{2,3},{3,4},{4,5},{5,6},{6,7},{7,8},{8,9},{9,10},{10,1... | collective-permute-start | bytes 1572872 | tf_op jit(solution)/shard_map/ppermute | solution.py:182
  457.5 14.5 %collective-permute-start.13 = (bf16[128,1,2048]{2,0,1:T(8,128)(2,1)S(1)}, bf16[128,1,2048]{2,0,1:T(8,128)(2,1)}, u32[]{:S(2)}, u32[]{:S(2)}) collective-permute-start(bf16[128,1,2048]{2,0,1:T(8,128)(2,1)S(1)} %collective-permute-done.12), channel_id=1, source_target_pairs={{0,1},{1,2},{2,3},{3,4},{4,5},{5,6},{6,7},{7,8},{8,9},{9,10},{10,1... | collective-permute-start | bytes 1572872 | tf_op jit(solution)/shard_map/ppermute | solution.py:182
  472.0 12.8 %collective-permute-start.14 = (bf16[128,1,2048]{2,0,1:T(8,128)(2,1)}, bf16[128,1,2048]{2,0,1:T(8,128)(2,1)}, u32[]{:S(2)}, u32[]{:S(2)}) collective-permute-start(bf16[128,1,2048]{2,0,1:T(8,128)(2,1)} %collective-permute-done.13), channel_id=1, source_target_pairs={{0,1},{1,2},{2,3},{3,4},{4,5},{5,6},{6,7},{7,8},{8,9},{9,10},{10,1... | collective-permute-start | bytes 1572872 | tf_op jit(solution)/shard_map/ppermute | solution.py:182
  525.5 157.4 %all-gather.8.cloned.1.call-start = ((), (), s32[]{:S(2)}) async-start(), calls=%async_computation.8 | async-start | bytes 8912896 | tf_op jit(solution)/shard_map/all_gather | solution.py:230
  612.7 252.0 %reduce-scatter.11.cloned.1.call-start = ((), (), s32[]{:S(2)}) async-start(), calls=%async_computation.10 | async-start | bytes 8912896 | tf_op jit(solution)/shard_map/reduce_scatter | solution.py:256
  746.1 181.5 %reduce-scatter.9.cloned.1.call-start = ((), (), s32[]{:S(2)}) async-start(), calls=%async_computation.9 | async-start | bytes 8912896 | tf_op jit(solution)/shard_map/reduce_scatter | solution.py:233
  768.0 26.4 %collective-permute-start.31 = (bf16[512,4,256]{2,0,1:T(8,128)(2,1)}, bf16[512,4,256]{2,0,1:T(8,128)(2,1)}, u32[]{:S(2)}, u32[]{:S(2)}) collective-permute-start(bf16[512,4,256]{2,0,1:T(8,128)(2,1)} %select_convert_fusion), channel_id=1, source_target_pairs={{0,64},{32,96},{64,0},{96,32},{1,65},{33,97},{65,1},{97,33},{2,66}... | collective-permute-start | bytes 3145736 | tf_op jit(solution)/shard_map/ppermute | solution.py:349
  779.4 36.3 %collective-permute-start.28 = (bf16[4,256,512]{2,1,0:T(8,128)(2,1)}, bf16[4,256,512]{2,1,0:T(8,128)(2,1)}, u32[]{:S(2)}, u32[]{:S(2)}) collective-permute-start(bf16[4,256,512]{2,1,0:T(8,128)(2,1)} %bitcast.57), channel_id=1, source_target_pairs={{0,64},{32,96},{64,0},{96,32},{1,65},{33,97},{65,1},{97,33},{2,66}... | collective-permute-start | bytes 3145736 | tf_op jit(solution)/shard_map/ppermute | solution.py:349
  796.5 21.1 %collective-permute-start.32 = (bf16[512,2,256]{2,0,1:T(8,128)(2,1)S(1)}, bf16[512,2,256]{2,0,1:T(8,128)(2,1)S(1)}, u32[]{:S(2)}, u32[]{:S(2)}) collective-permute-start(bf16[512,2,256]{2,0,1:T(8,128)(2,1)S(1)} %select_convert_fusion.3), channel_id=1, source_target_pairs={{0,32},{32,0},{64,96},{96,64},{1,33},{33,1},{65,97},{97,65},{2,34}... | collective-permute-start | bytes 1572872 | tf_op jit(solution)/shard_map/ppermute | solution.py:349
  818.6 10.9 %collective-permute-start.33 = (bf16[512,1,256]{2,0,1:T(8,128)(2,1)}, bf16[512,1,256]{2,0,1:T(8,128)(2,1)S(1)}, u32[]{:S(2)}, u32[]{:S(2)}) collective-permute-start(bf16[512,1,256]{2,0,1:T(8,128)(2,1)} %select_convert_fusion.5), channel_id=1, source_target_pairs={{0,16},{16,0},{1,17},{17,1},{2,18},{18,2},{3,19},{19,3},{4,20},{20... | collective-permute-start | bytes 786440 | tf_op jit(solution)/shard_map/ppermute | solution.py:349
  823.2 11.5 %collective-permute-start.30 = (bf16[1,256,512]{2,1,0:T(8,128)(2,1)S(1)}, bf16[1,256,512]{2,1,0:T(8,128)(2,1)S(1)}, u32[]{:S(2)}, u32[]{:S(2)}) collective-permute-start(bf16[1,256,512]{2,1,0:T(8,128)(2,1)S(1)} %select_convert_fusion.6), channel_id=1, source_target_pairs={{0,16},{16,0},{1,17},{17,1},{2,18},{18,2},{3,19},{19,3},{4,20},{20... | collective-permute-start | bytes 786440 | tf_op jit(solution)/shard_map/ppermute | solution.py:349
  844.4 10.1 %collective-permute-start.25 = (bf16[1,128,4,256]{3,1,2,0:T(8,128)(2,1)S(1)}, bf16[1,128,4,256]{3,1,2,0:T(8,128)(2,1)S(1)}, u32[]{:S(2)}, u32[]{:S(2)}) collective-permute-start(bf16[1,128,4,256]{3,1,2,0:T(8,128)(2,1)S(1)} %select_convert_fusion.7), channel_id=1, source_target_pairs={{0,64},{32,96},{64,0},{96,32},{1,65},{33,97},{65,1},{97,33},{2,66}... | collective-permute-start | bytes 786440 | tf_op jit(solution)/shard_map/ppermute | solution.py:349
  862.6 36.4 %collective-permute-start.22 = (bf16[4,256,3,1,128]{4,3,2,1,0:T(2,128)(2,1)S(1)}, bf16[4,256,3,1,128]{4,3,2,1,0:T(2,128)(2,1)}, u32[]{:S(2)}, u32[]{:S(2)}) collective-permute-start(bf16[4,256,3,1,128]{4,3,2,1,0:T(2,128)(2,1)S(1)} %copy.55), channel_id=1, source_target_pairs={{0,64},{32,96},{64,0},{96,32},{1,65},{33,97},{65,1},{97,33},{2,66}... | collective-permute-start | bytes 2359304 | tf_op jit(solution)/shard_map/ppermute | solution.py:349
  869.2 34.2 %collective-permute-start.15 = (f32[8,8,192]{2,0,1:T(8,128)S(1)}, f32[8,8,192]{2,0,1:T(8,128)S(1)}, u32[]{:S(2)}, u32[]{:S(2)}) collective-permute-start(f32[8,8,192]{2,0,1:T(8,128)S(1)} %slice_select_fusion.2), channel_id=1, source_target_pairs={{0,8},{1,9},{2,10},{3,11},{4,12},{5,13},{6,14},{7,15},{8,0},{9,1},... | collective-permute-start | bytes 147464 | tf_op jit(solution)/shard_map/ppermute | solution.py:349
  915.3 9.4 collective-permute-start.24
  917.1 9.0 collective-permute-start.19
  (131 other events, 2503.8 us)
Sparse Core Ops, SparseCore 0:
  12.4 73.0 all-gather.3
  87.6 70.3 all-gather.5
  161.4 84.6 reduce-scatter.4
  525.6 81.1 reduce-scatter.6
  612.9 70.0 all-gather.7
  746.2 84.7 reduce-scatter.10
  834.5 85.3 reduce-scatter.8
